TPU v7x, 256 devices: a whole 4x4x8 slice. The times are simulated.
256 devices in a mesh: stn: 64 (over y_hi, z, x), beam: 4 (over y_lo, core).
Axes of the slice: x: 4, y: 4 (y_hi: 2, y_lo: 2; y = y_hi * 2 + y_lo), z: 8, core: 2. Of those that a mesh axis runs over, the one named last changes fastest.
Arguments:
- voltages: bfloat16 [512, 2, 614400], P(('stn', 'beam')), may hold values from -6 to 6
- fir_taps: float32 [12, 8192], replicated, may hold values from -1.75 to 1.75
- delays: float32 [64, 64, 512], P('stn', 'beam'), may hold values from -16 to 16
- taper: float32 [64, 512], replicated, may hold values from 0.5 to 2
- station_map: int32 [512], replicated, may hold values from 0 to 511, each once
- beam_order: int32 [64], replicated, may hold values from 0 to 63, each once
- owners: int32 [4], replicated, may hold values from 0 to 63
Outputs:
- beams_re: float32 [64, 4096, 128], P('beam', 'stn')
- beams_im: float32 [64, 4096, 128], P('beam', 'stn')
Inputs may be any that keep to these rules, and one draw needn't show every extreme that they name: `station_map`: each station row holds a different physical station. `beam_order`: each beam slot forms a different beam.
All inputs are finite; a program needn't handle non-finite values.
Results may differ from a plain program's by a relative error of at most 0.0064.
Values may be sent and summed in bfloat16 or wider, within the bound.
No kernel may reach another device: no remote copies, remote signals or barrier semaphores. Data moves between devices by JAX's collectives and lax.ppermute only.
A program may use at most 128 MiB of HBM per device.

v0:
```python
import math
import jax
import jax.numpy as jnp
from jax import lax
from jax.sharding import PartitionSpec as P

P_SIZE = 64
Q = 128
CHANNELS = 4096
TWO_PI = 2.0 * math.pi


def from_root(value, axis, source):
    kept = jnp.where(lax.axis_index(axis) == source, value, 0).astype(value.dtype)
    return lax.psum(kept, axis)


def dft_tables():
    first_idx = jnp.arange(P_SIZE, dtype=jnp.int32)
    second_idx = jnp.arange(Q, dtype=jnp.int32)
    half_idx = jnp.arange(Q // 2, dtype=jnp.int32)
    first_angle = (
        TWO_PI / P_SIZE * (first_idx[:, None] * first_idx[None, :] % P_SIZE).astype(jnp.float32)
    )
    twist_angle = (
        TWO_PI / (P_SIZE * Q) * (first_idx[:, None] * second_idx[None, :]).astype(jnp.float32)
    )
    second_angle = TWO_PI / Q * (second_idx[:, None] * half_idx[None, :] % Q).astype(jnp.float32)
    return (
        jnp.cos(first_angle).astype(jnp.bfloat16),
        jnp.sin(first_angle).astype(jnp.bfloat16),
        jnp.cos(twist_angle),
        jnp.sin(twist_angle),
        jnp.cos(second_angle).astype(jnp.bfloat16),
        jnp.sin(second_angle).astype(jnp.bfloat16),
    )


def beam_weights(delay_cols, gain_cols, chan_ids):
    phase = (
        delay_cols[:, :, None]
        * chan_ids.astype(jnp.float32)[None, None, :]
        * (TWO_PI / (P_SIZE * Q))
    )
    weight_re = (gain_cols[:, :, None] * jnp.cos(phase)).astype(jnp.bfloat16)
    weight_im = (-(gain_cols[:, :, None] * jnp.sin(phase))).astype(jnp.bfloat16)
    left_re = jnp.concatenate((weight_re, -weight_im), axis=1)
    left_im = jnp.concatenate((weight_im, weight_re), axis=1)
    return (left_re, left_im)


def channelize(voltages, fir_taps):
    cos_one, sin_one, twist_cos, twist_sin, cos_two, sin_two = dft_tables()
    local_stations, pol_count, samples = voltages.shape
    tap_count, fft_width = fir_taps.shape
    frames = samples // fft_width - tap_count + 1
    blocks = voltages.reshape(local_stations, pol_count, frames + tap_count - 1, fft_width)
    filtered = jnp.zeros((local_stations, pol_count, frames, fft_width), jnp.float32)
    for tap_idx in range(tap_count):
        filtered = filtered + fir_taps[tap_idx] * blocks[:, :, tap_idx : tap_idx + frames].astype(
            jnp.float32
        )
    folded = filtered.astype(jnp.bfloat16).reshape(local_stations, pol_count, frames, P_SIZE, Q)
    first_table = jnp.concatenate((cos_one, -sin_one), axis=0)
    first_section = jnp.einsum(
        "spfnq,an->spfaq", folded, first_table, preferred_element_type=jnp.float32
    )
    first_re = first_section[:, :, :, :P_SIZE]
    first_im = first_section[:, :, :, P_SIZE:]
    turned = jnp.concatenate(
        (
            (first_re * twist_cos + first_im * twist_sin).astype(jnp.bfloat16),
            (first_im * twist_cos - first_re * twist_sin).astype(jnp.bfloat16),
        ),
        axis=4,
    )
    second_table = jnp.concatenate(
        (jnp.concatenate((cos_two, -sin_two), axis=1), jnp.concatenate((sin_two, cos_two), axis=1)),
        axis=0,
    )
    second = jnp.einsum("spfaq,qb->sbapf", turned, second_table, preferred_element_type=jnp.float32)
    half_q = Q // 2
    chan_re = (
        second[:, :half_q]
        .astype(jnp.bfloat16)
        .reshape(local_stations, half_q * P_SIZE, pol_count * frames)
    )
    chan_im = (
        second[:, half_q:]
        .astype(jnp.bfloat16)
        .reshape(local_stations, half_q * P_SIZE, pol_count * frames)
    )
    return jnp.stack((chan_re, chan_im), axis=0)


def combine(left_re, left_im, stacked_parts, beam_scale):
    stacked = jnp.concatenate((stacked_parts[0], stacked_parts[1]), axis=0)
    beam_re = (
        jnp.einsum("jrk,rkc->jkc", left_re, stacked, preferred_element_type=jnp.float32)
        * beam_scale
    )
    beam_im = (
        jnp.einsum("jrk,rkc->jkc", left_im, stacked, preferred_element_type=jnp.float32)
        * beam_scale
    )
    return jnp.stack((beam_re, beam_im), axis=0)


def on_device(voltages, fir_taps, delays, taper, station_map, beam_order, owners):
    stn_count = lax.axis_size("stn")
    beam_count = lax.axis_size("beam")
    stn_pos = lax.axis_index("stn")
    beam_pos = lax.axis_index("beam")
    local_stations = voltages.shape[0]
    stations = station_map.shape[0]
    group_beams = beam_order.shape[0] // beam_count
    chan_dev = CHANNELS // stn_count
    chan_ids = stn_pos * chan_dev + jnp.arange(chan_dev, dtype=jnp.int32)
    beam_scale = 1.0 / math.sqrt(P_SIZE * Q * stations)
    spectra = channelize(voltages, fir_taps)
    owner_model = from_root(delays, "stn", owners[beam_pos])[0]
    row_stn = jnp.arange(stn_count * local_stations, dtype=jnp.int32)
    all_rows = (
        (row_stn // local_stations * beam_count + jnp.arange(beam_count, dtype=jnp.int32)[:, None])
        * local_stations
        + row_stn % local_stations
    ).reshape(-1)
    phys_ids = station_map[all_rows]
    slot_gain = taper[beam_order[beam_pos * group_beams + jnp.arange(group_beams, dtype=jnp.int32)]]
    left_re, left_im = beam_weights(owner_model[:, phys_ids], slot_gain[:, phys_ids], chan_ids)
    full_rows = lax.all_gather(
        lax.all_to_all(spectra, "stn", split_axis=2, concat_axis=1, tiled=True),
        "beam",
        axis=1,
        tiled=True,
    )
    formed = combine(left_re, left_im, full_rows, beam_scale)
    return (formed[0], formed[1])


def solution(mesh):
    return jax.shard_map(
        on_device,
        mesh=mesh,
        in_specs=(P(("stn", "beam"), None, None), P(), P("stn", "beam", None), P(), P(), P(), P()),
        out_specs=(P("beam", "stn", None), P("beam", "stn", None)),
        check_vma=False,
    )
```

profile of v0, /device:TPU:16, one launch (start us, length us, event | category | flops | bytes accessed | tf_op | source)
XLA Modules:
  0.0 628.2 jit_solution(1775256071955894884)
XLA Ops:
  7.2 0.0 copy-start
  7.2 0.0 all-gather.2.cloned.1.call-start
  7.2 0.1 cosine_convert_fusion.1
  7.4 0.1 fusion.46
  7.5 0.1 fusion.41
  7.7 0.3 sine_convert_fusion
  7.9 0.3 fusion.49
  8.2 2.6 fusion.59
  10.9 6.3 reshape.166
  17.1 28.3 %add_convert_fusion.1 = bf16[2,2,64,8192]{3,2,1,0:T(8,128)(2,1)S(1)} fusion(bf16[2,2,75,8192]{3,2,1,0:T(8,128)(2,1)} %reshape.166, f32[8192]{0:T(1024)S(1)} %bitcast.83, f32[8192]{0:T(1024)S(1)} %bitcast.84, f32[8192]{0:T(1024)S(1)} %bitcast.74, f32[8192]{0:T(1024)S(1)} %bitcast.75, f32[8192]{0:T(1024)S(1)} %bitcast.76, f32[8192]{0:T(1024)S(1)} %bitcast.77, ...), kind=kLoop, calls=%fused_computation.16 | loop fusion | flops 75497472 | bytes 54919168 | tf_op jit(solution)/shard_map/convert_element_type | solution.py:63
  45.4 1.2 copy.38
  46.6 2.4 convolution_bitcast_fusion
  49.0 2.5 add_convert_fusion
  51.6 3.1 convert_bitcast_fusion
  54.7 4.3 fusion.58
  59.0 6.3 %copy.25 = bf16[2,64,64,2,64]{2,1,4,3,0:T(8,128)(2,1)} copy(bf16[2,64,64,2,64]{1,2,4,3,0:T(8,128)(2,1)} %get-tuple-element.12) | data formatting | bytes 4194304 | tf_op jit(solution)/shard_map/slice | solution.py:84
  65.3 5.7 stack_reshape.6
  71.0 6.4 %copy.26 = bf16[2,64,64,2,64]{2,1,4,3,0:T(8,128)(2,1)} copy(bf16[2,64,64,2,64]{1,2,4,3,0:T(8,128)(2,1)} %get-tuple-element.13) | data formatting | bytes 4194304 | tf_op jit(solution)/shard_map/slice | solution.py:89
  77.3 6.6 %stack_reshape.7 = bf16[1,2,4096,128]{2,3,1,0:T(8,128)(2,1)} reshape(bf16[2,64,64,2,64]{2,1,4,3,0:T(8,128)(2,1)} %copy.26) | data formatting | bytes 4194304 | tf_op jit(solution)/shard_map/stack;reshape | solution.py:93
  83.9 3.9 pad_maximum_fusion.3
  87.8 11.1 %copy.27 = bf16[2,2,4096,128]{3,1,0,2:T(2,128)(2,1)} copy(bf16[2,2,4096,128]{2,3,1,0:T(8,128)(2,1)} %pad_maximum_fusion.3) | data formatting | bytes 8388608 | tf_op jit(solution)/shard_map/stack | solution.py:93
  99.0 108.4 %all_to_all.18 = bf16[2,2,4096,128]{3,1,0,2:T(2,128)(2,1)S(1)} all-to-all(bf16[2,2,4096,128]{3,1,0,2:T(2,128)(2,1)} %copy.27), channel_id=1, replica_groups=mesh['stn'=64,'beam'=4] {'stn'}, dimensions={2} | all-to-all | bytes 8388608 | tf_op jit(solution)/shard_map/all_to_all | solution.py:132
  207.4 2.5 copy.28
  209.9 8.5 %copy.29 = bf16[2,64,2,64,128]{4,2,1,3,0:T(2,128)(2,1)} copy(bf16[2,64,2,64,128]{4,3,1,2,0:T(8,128)(2,1)} %bitcast.69) | data formatting | bytes 8388608 | tf_op jit(solution)/shard_map/all_to_all | solution.py:132
  218.4 0.0 all-gather.2.cloned.1.call-update
  218.4 0.0 copy-done.3
  218.4 0.1 copy.32
  218.5 0.0 copy-done.4
  218.6 0.6 dynamic_slice.3
  219.8 0.0 copy-done.1
  219.9 3.5 gather_fusion.2
  223.4 359.8 %psum.7 = f32[16,512]{0,1:T(8,128)S(1)} all-reduce(f32[16,512]{0,1:T(8,128)S(1)} %select_bitcast_fusion), channel_id=1, replica_groups=mesh['stn'=64,'beam'=4] {'stn'}, use_global_device_ids=true, to_apply=%region_0.1 | all-reduce | flops 8192 | bytes 65536 | tf_op jit(solution)/shard_map/psum | solution.py:15
  583.2 1.0 gather_fusion.4
  584.3 0.1 copy.33
  584.4 0.0 copy-done.2
  584.4 0.7 gather_fusion
  585.1 0.0 copy-done
  585.1 0.6 gather_fusion.1
  585.7 0.1 copy.30
  585.8 1.0 gather_fusion.3
  586.9 0.1 copy.31
  587.0 8.3 %fusion.57 = bf16[16,512,64]{1,0,2:T(8,128)(2,1)} fusion(f32[64]{0:T(128)S(1)} %add_convert_fusion.2, f32[16,512]{1,0:T(8,128)S(1)} %copy.33, f32[16,512]{1,0:T(8,128)S(1)} %copy.31), kind=kLoop, calls=%fused_computation.93 | loop fusion | flops 4194304 | bytes 1114368 | tf_op jit(solution)/shard_map/neg | solution.py:47
  595.3 9.2 %negate_convert_fusion = (bf16[16,512,64]{1,0,2:T(8,128)(2,1)}, bf16[16,512,64]{1,0,2:T(8,128)(2,1)}) fusion(f32[64]{0:T(128)S(1)} %add_convert_fusion.2, f32[16,512]{1,0:T(8,128)S(1)} %copy.33, f32[16,512]{1,0:T(8,128)S(1)} %copy.31), kind=kLoop, calls=%fused_computation.26 | loop fusion | flops 3670016 | bytes 2162944 | tf_op jit(solution)/shard_map/convert_element_type | solution.py:46
  604.5 6.6 %slice_bitcast_fusion.1 = (bf16[512,64,128]{2,0,1:T(8,128)(2,1)S(1)}, bf16[512,64,128]{2,0,1:T(8,128)(2,1)S(1)}) fusion(bf16[2,512,64,128]{3,1,2,0:T(8,128)(2,1)} %all-gather.2.cloned.1.call-done), kind=kLoop, calls=%fused_computation.9 | loop fusion | bytes 33554432 | tf_op jit(solution)/shard_map/squeeze | solution.py:97
  611.1 4.2 fusion.17
  615.3 1.0 copy.35
  616.2 4.2 fusion.23
  620.4 1.0 copy.34
  (17 shorter events, 0.1 us)
Async XLA Ops:
  7.2 577.9 %copy-start = (f32[64,512]{1,0:T(8,128)S(1)}, f32[64,512]{1,0:T(8,128)}, u32[]{:S(2)}) copy-start(f32[64,512]{1,0:T(8,128)} %param.10) | copy-start | bytes 393220
  7.2 597.3 %all-gather.2.cloned.1.call-start = ((), (), s32[]{:S(2)}) async-start(), calls=%async_computation.1 | async-start | bytes 20971520 | tf_op jit(solution)/shard_map/all_gather | solution.py:131
  209.9 8.5 %copy-start.3 = (f32[1,16,512]{2,1,0:T(8,128)S(1)}, f32[1,16,512]{2,1,0:T(8,128)}, u32[]{:S(2)}) copy-start(f32[1,16,512]{2,1,0:T(8,128)} %param.9) | copy-start | bytes 98308
  209.9 8.7 %copy-start.4 = (s32[4]{0:T(128)S(1)}, s32[4]{0:T(128)}, u32[]{:S(2)}) copy-start(s32[4]{0:T(128)} %param.13) | copy-start | bytes 52
  209.9 10.0 %copy-start.1 = (s32[512]{0:T(512)S(1)}, s32[512]{0:T(512)}, u32[]{:S(2)}) copy-start(s32[512]{0:T(512)} %param.11) | copy-start | bytes 6148
  209.9 374.5 %copy-start.2 = (s32[64]{0:T(128)S(1)}, s32[64]{0:T(128)}, u32[]{:S(2)}) copy-start(s32[64]{0:T(128)} %param.12) | copy-start | bytes 772
Sparse Core Ops, SparseCore 0:
  218.5 152.3 all-gather.1
where the time goes:
time: 629 us; the launch traced here: 628 us
  blocking collectives  468 us (74%)
  local copies, waits for them, and re-layouts  77.8 us (12%)
  other arithmetic  53.3 us (8%)
  between operations  14.9 us (2%)
  matrix products  13.9 us (2%)
    psum x1, blocking collectives, from_root(): return lax.psum(kept, axis)  360 us
    all_to_all x1, blocking collectives, on_device(): lax.all_to_all(spectra, 'stn', split_axis=2, concat_axis=1, tiled=True)  108 us
    convert_element_type x1, other arithmetic, channelize(): filtered.astype(jnp.bfloat16)  28.3 us
    another operation x3, local copies, waits for them, and re-layouts, channelize(): return jnp.stack((chan_re, chan_im), axis=0)  23.4 us
  transfers between devices with their start and end apart: 1, of which 0 were waited for; matrix products, arithmetic and copies ran while one was open for 4% of the time, Pallas kernels for 0%

commit v1 on v0

--- a/solution.py
+++ b/solution.py
@@ -12,7 +12,7 @@
 
 def from_root(value, axis, source):
     kept = jnp.where(lax.axis_index(axis) == source, value, 0).astype(value.dtype)
-    return lax.psum(kept, axis)
+    return lax.all_gather(kept, axis_name=axis).sum(axis=0)
 
 
 def dft_tables():

time: 629 us -> 428 us (0.68)
  blocking collectives: 468 us -> 0 us
  waiting for transfers between devices: 0.02 us -> 243 us
  starting transfers between devices: 0.04 us -> 14.8 us
    psum x1 -> x0, blocking collectives: 360 us -> none  [from_root(): return lax.psum(kept, axis)]
    all_gather x1, waiting for transfers between devices: 0.01 us -> 133 us  [on_device(): lax.all_gather(lax.all_to_all(spectra, 'stn', split_axis=2, concat_axis=1...]
    all_to_all x1 -> x0, blocking collectives: 108 us -> none  [on_device(): lax.all_to_all(spectra, 'stn', split_axis=2, concat_axis=1, tiled=True)]
    all_to_all x0 -> x1, waiting for transfers between devices: none -> 94.1 us  [on_device(): lax.all_to_all(spectra, 'stn', split_axis=2, concat_axis=1, tiled=True)]
    all_gather x0 -> x1, waiting for transfers between devices: none -> 16 us  [from_root(): return lax.all_gather(kept, axis_name=axis).sum(axis=0)]
    all_to_all x0 -> x1, starting transfers between devices: none -> 14.7 us  [on_device(): lax.all_to_all(spectra, 'stn', split_axis=2, concat_axis=1, tiled=True)]
  transfers between devices with their start and end apart: 1 -> 3, of which waited for: 0 -> 3; matrix products, arithmetic and copies ran while one was open for 4% -> 10% of each run, Pallas kernels for 0% -> 0%
where the time goes in v1:
time: 428 us; the launch traced here: 423 us
  waiting for transfers between devices  243 us (57%)
  local copies, waits for them, and re-layouts  80.4 us (19%)
  other arithmetic  56.4 us (13%)
  between operations  15 us (4%)
  starting transfers between devices  14.8 us (3%)
  matrix products  14 us (3%)
    all_gather x1, waiting for transfers between devices, on_device(): lax.all_gather(lax.all_to_all(spectra, 'stn', split_axis=2, concat_axis=1...  133 us
    all_to_all x1, waiting for transfers between devices, on_device(): lax.all_to_all(spectra, 'stn', split_axis=2, concat_axis=1, tiled=True)  94.1 us
    convert_element_type x1, other arithmetic, channelize(): filtered.astype(jnp.bfloat16)  29.1 us
    another operation x3, local copies, waits for them, and re-layouts, channelize(): return jnp.stack((chan_re, chan_im), axis=0)  23.4 us
    all_gather x1, waiting for transfers between devices, from_root(): return lax.all_gather(kept, axis_name=axis).sum(axis=0)  16 us
    all_to_all x1, starting transfers between devices, on_device(): lax.all_to_all(spectra, 'stn', split_axis=2, concat_axis=1, tiled=True)  14.7 us
    all_to_all x2, local copies, waits for them, and re-layouts, on_device(): lax.all_to_all(spectra, 'stn', split_axis=2, concat_axis=1, tiled=True)  13.4 us
    slice x2, local copies, waits for them, and re-layouts, channelize(): second[:, :half_q].astype(jnp.bfloat16)  10.6 us
  transfers between devices with their start and end apart: 3, of which 3 were waited for; matrix products, arithmetic and copies ran while one was open for 10% of the time, Pallas kernels for 0%

profile of v1, /device:TPU:16, one launch (start us, length us, event | category | flops | bytes accessed | tf_op | source)
XLA Modules:
  0.0 423.3 jit_solution(3262116013972345560)
XLA Ops:
  7.2 0.1 cosine_convert_fusion.1
  7.3 0.1 fusion.46
  7.5 0.1 fusion.41
  7.6 0.3 sine_convert_fusion
  7.9 0.3 fusion.49
  8.2 2.6 fusion.59
  10.8 6.3 %reshape.168 = bf16[2,2,75,8192]{3,2,1,0:T(8,128)(2,1)} reshape(bf16[2,2,614400]{2,1,0:T(2,128)(2,1)} %param.7) | data formatting | bytes 9830400 | tf_op jit(solution)/shard_map/reshape | solution.py:57
  17.1 29.1 %add_convert_fusion.1 = bf16[2,2,64,8192]{3,2,1,0:T(8,128)(2,1)S(1)} fusion(bf16[2,2,75,8192]{3,2,1,0:T(8,128)(2,1)} %reshape.168, f32[8192]{0:T(1024)S(1)} %bitcast.81, f32[8192]{0:T(1024)S(1)} %bitcast.82, f32[8192]{0:T(1024)S(1)} %bitcast.72, f32[8192]{0:T(1024)S(1)} %bitcast.73, f32[8192]{0:T(1024)S(1)} %bitcast.74, f32[8192]{0:T(1024)S(1)} %bitcast.75, ...), kind=kLoop, calls=%fused_computation.16 | loop fusion | flops 75497472 | bytes 54919168 | tf_op jit(solution)/shard_map/convert_element_type | solution.py:63
  46.2 1.2 copy.36
  47.4 2.5 convolution_bitcast_fusion
  49.8 2.5 add_convert_fusion
  52.3 3.1 convert_bitcast_fusion
  55.5 4.3 %fusion.58 = (bf16[2,64,64,2,64]{1,2,4,3,0:T(8,128)(2,1)}, bf16[2,64,64,2,64]{1,2,4,3,0:T(8,128)(2,1)}) fusion(bf16[2,128,64,2,64]{1,2,4,3,0:T(8,128)(2,1)S(1)} %convert_bitcast_fusion), kind=kLoop, calls=%fused_computation.94 | loop fusion | bytes 8388608 | tf_op jit(solution)/shard_map/slice | solution.py:84
  59.7 6.3 %copy.23 = bf16[2,64,64,2,64]{2,1,4,3,0:T(8,128)(2,1)} copy(bf16[2,64,64,2,64]{1,2,4,3,0:T(8,128)(2,1)} %get-tuple-element.12) | data formatting | bytes 4194304 | tf_op jit(solution)/shard_map/slice | solution.py:84
  66.1 5.7 %stack_reshape.6 = bf16[1,2,4096,128]{2,3,1,0:T(8,128)(2,1)S(1)} reshape(bf16[2,64,64,2,64]{2,1,4,3,0:T(8,128)(2,1)} %copy.23) | data formatting | bytes 4194304 | tf_op jit(solution)/shard_map/stack;reshape | solution.py:93
  71.7 6.3 %copy.24 = bf16[2,64,64,2,64]{2,1,4,3,0:T(8,128)(2,1)} copy(bf16[2,64,64,2,64]{1,2,4,3,0:T(8,128)(2,1)} %get-tuple-element.13) | data formatting | bytes 4194304 | tf_op jit(solution)/shard_map/slice | solution.py:89
  78.1 6.6 %stack_reshape.7 = bf16[1,2,4096,128]{2,3,1,0:T(8,128)(2,1)} reshape(bf16[2,64,64,2,64]{2,1,4,3,0:T(8,128)(2,1)} %copy.24) | data formatting | bytes 4194304 | tf_op jit(solution)/shard_map/stack;reshape | solution.py:93
  84.7 3.9 pad_maximum_fusion.3
  88.6 11.2 %copy.25 = bf16[2,2,4096,128]{3,1,0,2:T(2,128)(2,1)} copy(bf16[2,2,4096,128]{2,3,1,0:T(8,128)(2,1)} %pad_maximum_fusion.3) | data formatting | bytes 8388608 | tf_op jit(solution)/shard_map/stack | solution.py:93
  99.8 14.7 %all-to-all-start = ((bf16[2,2,4096,128]{3,1,0,2:T(2,128)(2,1)}), bf16[2,2,4096,128]{3,1,0,2:T(2,128)(2,1)}, u32[]{:S(2)}, u32[]{:S(2)}) async-start(bf16[2,2,4096,128]{3,1,0,2:T(2,128)(2,1)} %copy.25), calls=%async_computation | async-start | bytes 8388608 | tf_op jit(solution)/shard_map/all_to_all | solution.py:132
  114.6 0.0 all-gather.6.cloned.1.call-start
  114.6 0.6 dynamic_slice.3
  115.9 0.6 broadcast_select_fusion
  116.5 0.0 all-gather.6.cloned.1.call-update
  116.5 0.0 all-gather.4.cloned.1.call-start
  116.6 94.1 %all-to-all-done = bf16[2,2,4096,128]{3,1,0,2:T(2,128)(2,1)} async-done(((bf16[2,2,4096,128]{3,1,0,2:T(2,128)(2,1)}), bf16[2,2,4096,128]{3,1,0,2:T(2,128)(2,1)}, u32[]{:S(2)}, u32[]{:S(2)}) %all-to-all-start) | async-done | bytes 4194336 | tf_op jit(solution)/shard_map/all_to_all | solution.py:132
  210.7 4.7 %copy.26 = bf16[2,2,4096,128]{3,2,1,0:T(8,128)(2,1)} copy(bf16[2,2,4096,128]{3,1,0,2:T(2,128)(2,1)} %all-to-all-done) | data formatting | bytes 8388608 | tf_op jit(solution)/shard_map/all_to_all | solution.py:132
  215.4 8.6 %copy.27 = bf16[2,64,2,64,128]{4,2,1,3,0:T(2,128)(2,1)} copy(bf16[2,64,2,64,128]{4,3,1,2,0:T(8,128)(2,1)} %bitcast.67) | data formatting | bytes 8388608 | tf_op jit(solution)/shard_map/all_to_all | solution.py:132
  224.0 0.0 all-gather.4.cloned.1.call-update
  224.1 0.7 gather_fusion
  224.8 0.6 gather_fusion.1
  225.4 0.1 copy.28
  225.6 3.7 gather_fusion.2
  229.3 1.0 gather_fusion.3
  230.4 0.1 copy.29
  230.5 16.0 %all-gather.6.cloned.1.call-done = f32[64,16,512]{2,1,0:T(8,128)} async-done(((f32[1,16,512]{2,1,0:T(8,128)}), f32[64,16,512]{2,1,0:T(8,128)}) %all-gather.6.cloned.1.call-update) | async-done | bytes 2097168 | tf_op jit(solution)/shard_map/all_gather | solution.py:15
  246.5 1.7 reduce.1
  248.2 0.1 copy.30
  248.3 1.0 gather_fusion.4
  249.4 0.1 copy.31
  249.5 8.3 %fusion.57 = bf16[16,512,64]{1,0,2:T(8,128)(2,1)} fusion(f32[64]{0:T(128)S(1)} %add_convert_fusion.2, f32[16,512]{1,0:T(8,128)S(1)} %copy.31, f32[16,512]{1,0:T(8,128)S(1)} %copy.29), kind=kLoop, calls=%fused_computation.93 | loop fusion | flops 4194304 | bytes 1114368 | tf_op jit(solution)/shard_map/neg | solution.py:47
  257.8 9.2 %negate_convert_fusion = (bf16[16,512,64]{1,0,2:T(8,128)(2,1)}, bf16[16,512,64]{1,0,2:T(8,128)(2,1)}) fusion(f32[64]{0:T(128)S(1)} %add_convert_fusion.2, f32[16,512]{1,0:T(8,128)S(1)} %copy.31, f32[16,512]{1,0:T(8,128)S(1)} %copy.29), kind=kLoop, calls=%fused_computation.26 | loop fusion | flops 3670016 | bytes 2162944 | tf_op jit(solution)/shard_map/convert_element_type | solution.py:46
  267.0 132.5 %all-gather.4.cloned.1.call-done = bf16[2,512,64,128]{3,1,2,0:T(8,128)(2,1)} async-done(((bf16[2,128,64,128]{3,1,2,0:T(8,128)(2,1)}), bf16[2,512,64,128]{3,1,2,0:T(8,128)(2,1)}) %all-gather.4.cloned.1.call-update) | async-done | bytes 16777232 | tf_op jit(solution)/shard_map/all_gather | solution.py:131
  399.5 6.6 %slice_bitcast_fusion.1 = (bf16[512,64,128]{2,0,1:T(8,128)(2,1)S(1)}, bf16[512,64,128]{2,0,1:T(8,128)(2,1)S(1)}) fusion(bf16[2,512,64,128]{3,1,2,0:T(8,128)(2,1)} %all-gather.4.cloned.1.call-done), kind=kLoop, calls=%fused_computation.9 | loop fusion | bytes 33554432 | tf_op jit(solution)/shard_map/squeeze | solution.py:97
  406.1 4.2 fusion.17
  410.3 1.0 copy.33
  411.3 4.2 fusion.23
  415.5 1.0 copy.32
  (23 shorter events, 0.1 us)
Async XLA Ops:
  7.2 217.6 %copy-start = (f32[64,512]{1,0:T(8,128)S(1)}, f32[64,512]{1,0:T(8,128)}, u32[]{:S(2)}) copy-start(f32[64,512]{1,0:T(8,128)} %param.10) | copy-start | bytes 393220
  88.6 26.0 %copy-start.5 = (s32[4]{0:T(128)S(1)}, s32[4]{0:T(128)}, u32[]{:S(2)}) copy-start(s32[4]{0:T(128)} %param.13) | copy-start | bytes 52
  88.6 27.2 %copy-start.4 = (f32[1,16,512]{2,1,0:T(8,128)S(1)}, f32[1,16,512]{2,1,0:T(8,128)}, u32[]{:S(2)}) copy-start(f32[1,16,512]{2,1,0:T(8,128)} %param.9) | copy-start | bytes 98308
  99.8 110.9 %all-to-all-start = ((bf16[2,2,4096,128]{3,1,0,2:T(2,128)(2,1)}), bf16[2,2,4096,128]{3,1,0,2:T(2,128)(2,1)}, u32[]{:S(2)}, u32[]{:S(2)}) async-start(bf16[2,2,4096,128]{3,1,0,2:T(2,128)(2,1)} %copy.25), calls=%async_computation | async-start | bytes 8388608 | tf_op jit(solution)/shard_map/all_to_all | solution.py:132
  114.6 131.9 %all-gather.6.cloned.1.call-start = ((), (), s32[]{:S(2)}) async-start(), calls=%async_computation.2 | async-start | bytes 2129920 | tf_op jit(solution)/shard_map/all_gather | solution.py:15
  116.5 283.0 %all-gather.4.cloned.1.call-start = ((), (), s32[]{:S(2)}) async-start(), calls=%async_computation.1 | async-start | bytes 20971520 | tf_op jit(solution)/shard_map/all_gather | solution.py:131
  215.4 8.7 %copy-start.3 = (s32[64]{0:T(128)S(1)}, s32[64]{0:T(128)}, u32[]{:S(2)}) copy-start(s32[64]{0:T(128)} %param.12) | copy-start | bytes 772
  215.4 10.2 %copy-start.2 = (s32[512]{0:T(512)S(1)}, s32[512]{0:T(512)}, u32[]{:S(2)}) copy-start(s32[512]{0:T(512)} %param.11) | copy-start | bytes 6148
  411.3 5.2 %copy-start.1 = (f32[64,512]{1,0:T(8,128)S(1)}, f32[64,512]{1,0:T(8,128)}, u32[]{:S(2)}) copy-start(f32[64,512]{1,0:T(8,128)} %param.10) | copy-start | bytes 393220
Sparse Core Ops, SparseCore 0:
  119.5 126.9 all-gather.5
  248.3 151.1 all-gather.3
